TPU v7x, 128 devices: a whole 4x4x4 slice. The times are simulated.
128 devices in a mesh: expert: 8 (over y_lo, x), tile: 16 (over z, y_hi, core).
Axes of the slice: x: 4, y: 4 (y_hi: 2, y_lo: 2; y = y_hi * 2 + y_lo), z: 4, core: 2. Of those that a mesh axis runs over, the one named last changes fastest.
Arguments:
- activations: bfloat16 [6144, 6144], P(('expert', 'tile')), may hold values from -40 to 40
- expert_ids: int32 [6144, 2], P(('expert', 'tile')), may hold values from 0 to 7, all different within a row; in each aligned block of 48 rows (0 to 47, 48 to 95, ...) at most 24 rows name the same one
Outputs:
- hessian: float32 [8, 6144, 6144], P('expert', 'tile')
- panels: float32 [8, 6144, 1536], P('expert', 'tile')
Inputs may be any that keep to these rules, and one draw needn't show every extreme that they name: `expert_ids`: each row names 2 different experts; within the rows of one device no expert is named more than 24 times, a bound that some block reaches; every expert is named by some row.
All inputs are finite; a program needn't handle non-finite values.
Results may differ from a plain program's by a relative error of at most 0.0003.
Values may be sent and summed in bfloat16 or wider, within the bound.
No kernel may reach another device: no remote copies, remote signals or barrier semaphores. Data moves between devices by JAX's collectives and lax.ppermute only.
A program may use at most 256 MiB of HBM per device.

v0:
```python
import math
import jax
import jax.numpy as jnp
from jax import lax
from jax.sharding import PartitionSpec as P

PANEL = 768
damp_fraction = 0.01


def side_by_side(arrays, axis, split_dim, concat_dim, along):
    widths = [math.prod(a.shape[along:]) for a in arrays]
    both = jnp.concatenate(
        [a.reshape(*a.shape[:along], w) for a, w in zip(arrays, widths)], axis=along
    )
    out = lax.all_to_all(both, axis, split_axis=split_dim, concat_axis=concat_dim, tiled=True)
    blocks = jnp.split(out, [sum(widths[:k]) for k in range(1, len(widths))], axis=along)
    return tuple((b.reshape(*out.shape[:along], *a.shape[along:]) for a, b in zip(arrays, blocks)))


def copy_for_each(x, axis):
    count = lax.axis_size(axis)
    return lax.all_to_all(jnp.broadcast_to(x[None], (count, *x.shape)), axis, 0, 0, tiled=True)


def taken_together(x, axis):
    return copy_for_each(x, axis).sum(axis=0)


def local(activations, expert_ids):
    tile_count = lax.axis_size("tile")
    group_count = lax.axis_size("expert")
    token_count = activations.shape[0]
    feature_width = activations.shape[1]
    capacity = 2 * token_count * expert_ids.shape[1] // group_count
    rows_device = feature_width // tile_count
    tile_index = lax.axis_index("tile")
    expert_iota = jnp.arange(group_count, dtype=jnp.int32)
    global_rows = tile_index * rows_device + jnp.arange(rows_device, dtype=jnp.int32)
    routed = jnp.sum((expert_ids[None][..., None] == expert_iota).astype(jnp.int32), axis=2)
    slot_index = jnp.cumsum(routed, axis=1) - 1
    slot_iota = jnp.arange(capacity, dtype=jnp.int32)
    selector = (routed[..., None] > 0) & (slot_index[..., None] == slot_iota)
    packed = jnp.einsum(
        "nkes,nkd->ensd",
        selector.astype(jnp.bfloat16),
        activations[None],
        preferred_element_type=jnp.float32,
    ).astype(jnp.bfloat16)
    flags = jnp.transpose(jnp.sum(selector.astype(jnp.float32), axis=1), (1, 0, 2)).astype(
        jnp.bfloat16
    )
    send_rows = packed
    send_flags = flags
    send_rows = send_rows.reshape(group_count, capacity, feature_width)
    send_flags = send_flags.reshape(group_count, capacity)
    received_rows, received_flags = side_by_side((send_rows, send_flags), "expert", 0, 0, 2)
    accumulate_received_rows = lax.all_gather(
        received_rows.reshape(group_count * capacity, feature_width), "tile", axis=0, tiled=True
    )
    accumulate_received_flags = lax.all_gather(
        received_flags.reshape(group_count * capacity), "tile", axis=0, tiled=True
    )
    own_columns = lax.dynamic_slice_in_dim(
        accumulate_received_rows, tile_index * rows_device, rows_device, 1
    )
    total = jnp.einsum(
        "tr,tc->rc", own_columns, accumulate_received_rows, preferred_element_type=jnp.float32
    )
    expert_count = jnp.sum(accumulate_received_flags.astype(jnp.float32))
    hessian = total * (2.0 / expert_count)
    diag_mask = global_rows[:, None] == jnp.arange(feature_width, dtype=jnp.int32)[None, :]
    diag_total = taken_together(jnp.sum(jnp.where(diag_mask, hessian, jnp.float32(0.0))), "tile")
    damping = damp_fraction * diag_total / feature_width
    hessian = hessian + jnp.where(diag_mask, damping, jnp.float32(0.0))

    def panel_rows_fetch(members, panel_start):
        placement = (
            panel_start + jnp.arange(PANEL, dtype=jnp.int32)[:, None] == global_rows[None, :]
        ).astype(jnp.float32)
        placed = tuple(
            (
                jnp.dot(placement, member_rows, precision=lax.Precision.HIGHEST)
                for member_rows in members
            )
        )
        return lax.psum(placed, "tile")

    factors = []
    for panel in range(2):
        panel_start = panel * PANEL
        panel_block = hessian[:, panel_start : panel_start + PANEL]
        if factors:
            diagonal_rows, earlier_rows = panel_rows_fetch((panel_block, factors[0]), panel_start)
            panel_block = panel_block - jnp.dot(
                factors[0], earlier_rows.T, precision=lax.Precision.HIGHEST
            )
            diagonal_block = diagonal_rows - jnp.dot(
                earlier_rows, earlier_rows.T, precision=lax.Precision.HIGHEST
            )
        else:
            diagonal_block = panel_rows_fetch((panel_block,), panel_start)[0]
        diagonal_factor = jnp.linalg.cholesky(diagonal_block)
        panel_factor = jax.scipy.linalg.solve_triangular(
            diagonal_factor, panel_block.T, lower=True
        ).T
        column_index = panel_start + jnp.arange(PANEL, dtype=jnp.int32)
        lower_mask = global_rows[:, None] >= column_index[None, :]
        factors.append(jnp.where(lower_mask, panel_factor, jnp.float32(0.0)))
    return (hessian[None], jnp.concatenate(factors, axis=1)[None])


def solution(mesh):
    placed = (P(("expert", "tile"), None), P(("expert", "tile"), None))
    return jax.shard_map(
        local,
        mesh=mesh,
        in_specs=placed,
        out_specs=(P("expert", "tile", None), P("expert", "tile", None)),
        check_vma=False,
    )
```

profile of v0, /device:TPU:0, one launch (start us, length us, event | category | flops | bytes accessed | tf_op | source)
XLA Modules:
  0.0 1108.4 jit_solution(1316372026263907840)
XLA Ops:
  9.4 36.0 %all_to_all.11 = bf16[8,24,6145]{2,1,0:T(8,128)(2,1)S(1)} all-to-all(bf16[8,24,6145]{2,1,0:T(8,128)(2,1)S(1)} %pad_maximum_fusion), channel_id=1, replica_groups=mesh['expert'=8,'tile'=16] {'expert'}, dimensions={0} | all-to-all | bytes 4719360 | tf_op jit(solution)/shard_map/all_to_all | solution.py:16
  49.4 39.8 %all-reduce.1 = bf16[3072]{0:T(1024)(128)(2,1)S(1)} all-reduce(bf16[3072]{0:T(1024)(128)(2,1)S(1)} %dynamic-update-slice.25), channel_id=1, replica_groups=mesh['expert'=8,'tile'=16] {'tile'}, use_global_device_ids=true, to_apply=%add.1 | all-reduce | flops 3072 | bytes 12288
  90.5 162.6 %all-gather.2.cloned.1.call-done = bf16[3072,6144]{1,0:T(8,128)(2,1)} async-done(((bf16[192,6144]{1,0:T(8,128)(2,1)}), bf16[3072,6144]{1,0:T(8,128)(2,1)}) %all-gather.2.cloned.1.call-update) | async-done | bytes 37748752 | tf_op jit(solution)/shard_map/all_gather | solution.py:58
  253.1 24.3 %select_reduce_fusion = (f32[]{:T(128)}, f32[384,6144]{1,0:T(8,128)}) fusion(s32[384]{0:T(512)S(1)} %iota_add_fusion.1, f32[]{:T(128)S(6)} %div.12, bf16[3072,6144]{1,0:T(8,128)(2,1)} %all-gather.2.cloned.1.call-done, s32[]{:T(128)S(6)} %select_n.21), kind=kOutput, calls=%fused_computation.5 | convolution fusion | flops 14504951808 | bytes 49546764 | tf_op jit(solution)/shard_map/tr,tc->rc/dot_general | solution.py:67
  302.8 10.6 all-reduce.8.cloned.1.call-start
  320.8 127.3 %all-reduce.6.cloned.1.call-done = f32[768,768]{0,1:T(8,128)} async-done(((f32[768,768]{0,1:T(8,128)}), f32[768,768]{0,1:T(8,128)}) %all-reduce.6.cloned.1.call-update) | async-done | bytes 2359312 | tf_op jit(solution)/shard_map/psum | solution.py:87
  454.7 11.7 %cholesky.453 = f32[128,128]{1,0:T(8,128)S(1)} custom-call(f32[128,128]{1,0:T(8,128)S(1)} %cholesky.669), custom_call_target="Cholesky" | custom-call | tf_op jit(solution)/shard_map/jit(cholesky)/cholesky | solution.py:103
  479.2 11.7 %cholesky.472 = f32[128,128]{1,0:T(8,128)S(1)} custom-call(f32[128,128]{1,0:T(8,128)S(1)} %cholesky.673), custom_call_target="Cholesky" | custom-call | tf_op jit(solution)/shard_map/jit(cholesky)/cholesky | solution.py:103
  491.0 10.2 custom-call.42
  503.1 11.7 %cholesky.493 = f32[128,128]{1,0:T(8,128)S(1)} custom-call(f32[128,128]{1,0:T(8,128)S(1)} %cholesky.678), custom_call_target="Cholesky" | custom-call | tf_op jit(solution)/shard_map/jit(cholesky)/cholesky | solution.py:103
  527.2 11.9 %cholesky.512 = f32[128,128]{1,0:T(8,128)S(1)} custom-call(f32[128,128]{1,0:T(8,128)S(1)} %cholesky.683), custom_call_target="Cholesky" | custom-call | tf_op jit(solution)/shard_map/jit(cholesky)/cholesky | solution.py:103
  551.4 11.7 %cholesky.531 = f32[128,128]{1,0:T(8,128)S(1)} custom-call(f32[128,128]{1,0:T(8,128)S(1)} %cholesky.688), custom_call_target="Cholesky" | custom-call | tf_op jit(solution)/shard_map/jit(cholesky)/cholesky | solution.py:103
  575.1 12.1 %cholesky.548 = f32[128,128]{1,0:T(8,128)S(1)} custom-call(f32[128,128]{1,0:T(8,128)S(1)} %convolution_subtract_fusion.21), custom_call_target="Cholesky" | custom-call | tf_op jit(solution)/shard_map/jit(cholesky)/cholesky | solution.py:103
  593.9 17.5 %while.4 = (s32[]{:T(128)}, f32[768,768]{1,0:T(8,128)}, s32[6,2]{0,1:T(2,128)S(1)}, f32[6,128,128]{2,1,0:T(8,128)S(1)}, s32[]{:T(128)}) while((s32[]{:T(128)}, f32[768,768]{1,0:T(8,128)}, s32[6,2]{0,1:T(2,128)S(1)}, f32[6,128,128]{2,1,0:T(8,128)S(1)}, s32[]{:T(128)}) %tuple.86), condition=%wide.while_cond, body=%wide.while_body.sunk | while | flops 2 | bytes 131181 | solution.py:104
  611.5 59.0 %custom-call.46 = f32[6,128,128]{1,2,0:T(8,128)S(1)} custom-call(f32[6,128,128]{2,1,0:T(8,128)S(1)} %get-tuple-element.18), custom_call_target="InvertDiagBlocksLowerTriangular" | custom-call | tf_op jit(solution)/shard_map/jit(_solve_triangular)/triangular_solve | solution.py:104
  697.3 151.3 %all-reduce.8.cloned.1.call-done = (f32[768,768]{1,0:T(8,128)}, f32[768,768]{0,1:T(8,128)}) async-done(((f32[768,768]{1,0:T(8,128)}, f32[768,768]{0,1:T(8,128)}), (f32[768,768]{1,0:T(8,128)}, f32[768,768]{0,1:T(8,128)})) %all-reduce.8.cloned.1.call-update) | async-done | bytes 4718608 | tf_op jit(solution)/shard_map/psum | solution.py:87
  869.1 11.7 %cholesky.563 = f32[128,128]{1,0:T(8,128)S(1)} custom-call(f32[128,128]{1,0:T(8,128)S(1)} %cholesky.692), custom_call_target="Cholesky" | custom-call | tf_op jit(solution)/shard_map/jit(cholesky)/cholesky | solution.py:103
  893.6 11.7 %cholesky.582 = f32[128,128]{1,0:T(8,128)S(1)} custom-call(f32[128,128]{1,0:T(8,128)S(1)} %cholesky.696), custom_call_target="Cholesky" | custom-call | tf_op jit(solution)/shard_map/jit(cholesky)/cholesky | solution.py:103
  918.8 11.7 %cholesky.603 = f32[128,128]{1,0:T(8,128)S(1)} custom-call(f32[128,128]{1,0:T(8,128)S(1)} %cholesky.701), custom_call_target="Cholesky" | custom-call | tf_op jit(solution)/shard_map/jit(cholesky)/cholesky | solution.py:103
  942.9 11.8 %cholesky.622 = f32[128,128]{1,0:T(8,128)S(1)} custom-call(f32[128,128]{1,0:T(8,128)S(1)} %cholesky.706), custom_call_target="Cholesky" | custom-call | tf_op jit(solution)/shard_map/jit(cholesky)/cholesky | solution.py:103
  967.0 11.7 %cholesky.641 = f32[128,128]{1,0:T(8,128)S(1)} custom-call(f32[128,128]{1,0:T(8,128)S(1)} %cholesky.711), custom_call_target="Cholesky" | custom-call | tf_op jit(solution)/shard_map/jit(cholesky)/cholesky | solution.py:103
  990.7 11.9 %cholesky.658 = f32[128,128]{1,0:T(8,128)S(1)} custom-call(f32[128,128]{1,0:T(8,128)S(1)} %convolution_subtract_fusion.20), custom_call_target="Cholesky" | custom-call | tf_op jit(solution)/shard_map/jit(cholesky)/cholesky | solution.py:103
  1008.6 17.9 %while.5 = (s32[]{:T(128)}, f32[768,768]{1,0:T(8,128)}, s32[6,2]{0,1:T(2,128)S(1)}, f32[6,128,128]{2,1,0:T(8,128)S(1)}, s32[]{:T(128)}) while((s32[]{:T(128)}, f32[768,768]{1,0:T(8,128)}, s32[6,2]{0,1:T(2,128)S(1)}, f32[6,128,128]{2,1,0:T(8,128)S(1)}, s32[]{:T(128)}) %tuple.99), condition=%wide.while_cond.clone, body=%wide.while_body.clone.sunk | while | flops 2 | bytes 131181 | solution.py:104
  1026.5 59.0 %custom-call.52 = f32[6,128,128]{1,2,0:T(8,128)S(1)} custom-call(f32[6,128,128]{2,1,0:T(8,128)S(1)} %get-tuple-element.19), custom_call_target="InvertDiagBlocksLowerTriangular" | custom-call | tf_op jit(solution)/shard_map/jit(_solve_triangular)/triangular_solve | solution.py:104
  (198 shorter events, 262.7 us)
Async XLA Ops:
  7.2 1.2 copy-start
  7.2 245.9 %all-gather.2.cloned.1.call-start = ((), (), s32[]{:S(2)}) async-start(), calls=%async_computation.2 | async-start | bytes 40108032 | tf_op jit(solution)/shard_map/all_gather | solution.py:58
  47.1 0.7 copy-start.12
  278.5 10.9 all-to-all-start.1
  282.0 166.1 %all-reduce.6.cloned.1.call-start = ((), (), s32[]{:S(2)}) async-start(), calls=%async_computation.3 | async-start | bytes 4718592 | tf_op jit(solution)/shard_map/psum | solution.py:87
  295.6 3.6 copy-start.2
  302.8 545.7 %all-reduce.8.cloned.1.call-start = ((), (), s32[]{:S(2)}) async-start(), calls=%async_computation.4 | async-start | bytes 9437184 | tf_op jit(solution)/shard_map/psum | solution.py:87
  448.1 3.2 copy-start.6
  453.3 1.4 copy-start.8
  593.9 79.7 %copy-start.9 = (f32[768,384]{0,1:T(8,128)S(1)}, f32[768,384]{0,1:T(8,128)}, u32[]{:S(2)}) copy-start(f32[768,384]{0,1:T(8,128)} %slice_bitcast_fusion) | copy-start | bytes 3538948
  684.2 164.3 %copy-start.4 = (f32[384,768]{0,1:T(8,128)}, f32[384,768]{0,1:T(8,128)S(1)}, u32[]{:S(2)}) copy-start(f32[384,768]{0,1:T(8,128)S(1)} %bitcast_select_fusion.1) | copy-start | bytes 3538948
  848.6 9.0 copy-start.3
  848.6 9.0 copy-start.11
  867.7 1.4 copy-start.7
  1008.6 80.1 %copy-start.10 = (f32[768,384]{0,1:T(8,128)S(1)}, f32[768,384]{0,1:T(8,128)}, u32[]{:S(2)}) copy-start(f32[768,384]{0,1:T(8,128)} %fusion.7) | copy-start | bytes 3538948
  1096.1 3.4 copy-start.5
  1099.5 2.1 copy-start.1
Sparse Core Ops, SparseCore 0:
  47.2 205.8 all-gather.1
  303.0 145.0 all-reduce.5
  687.9 160.6 all-reduce.7
where the time goes:
time: 1120 us; the launch traced here: 1110 us
  waiting for transfers between devices  449 us (40%)
  other arithmetic  390 us (35%)
  matrix products  98.9 us (9%)
  blocking collectives  75.8 us (7%)
  local copies, waits for them, and re-layouts  56.5 us (5%)
  between operations  24.1 us (2%)
  starting transfers between devices  14.1 us (1%)
    psum x2, waiting for transfers between devices, panel_rows_fetch(): return lax.psum(placed, 'tile')  279 us
    another operation x45, other arithmetic, local(): diagonal_factor = jnp.linalg.cholesky(diagonal_block)  248 us
    all_gather x1, waiting for transfers between devices, local(): lax.all_gather(received_rows.reshape(group_count * capacity, feature_widt...  163 us
    another operation x5, other arithmetic, local(): jax.scipy.linalg.solve_triangular(diagonal_factor, panel_block.T, lower=T...  121 us
    unnamed x1, blocking collectives  39.8 us
    all_to_all x1, blocking collectives, side_by_side(): lax.all_to_all(both, axis, split_axis=split_dim, concat_axis=concat_dim,...  36 us
    another operation x39, local copies, waits for them, and re-layouts, local(): jax.scipy.linalg.solve_triangular(diagonal_factor, panel_block.T, lower=T...  35.3 us
    another operation x22, matrix products, local(): jax.scipy.linalg.solve_triangular(diagonal_factor, panel_block.T, lower=T...  27.3 us
  transfers between devices with their start and end apart: 4, of which 4 were waited for; matrix products, arithmetic and copies ran while one was open for 2% of the time, Pallas kernels for 0%

commit v1 on v0

--- a/solution.py
+++ b/solution.py
@@ -55,8 +55,17 @@
     send_rows = send_rows.reshape(group_count, capacity, feature_width)
     send_flags = send_flags.reshape(group_count, capacity)
     received_rows, received_flags = side_by_side((send_rows, send_flags), "expert", 0, 0, 2)
-    accumulate_received_rows = lax.all_gather(
-        received_rows.reshape(group_count * capacity, feature_width), "tile", axis=0, tiled=True
+    accumulate_received_rows = jnp.concatenate(
+        lax.all_to_all(
+            jnp.stack(
+                [received_rows.reshape(group_count * capacity, feature_width)]
+                * lax.axis_size("tile")
+            ),
+            "tile",
+            0,
+            0,
+        ),
+        axis=0,
     )
     accumulate_received_flags = lax.all_gather(
         received_flags.reshape(group_count * capacity), "tile", axis=0, tiled=True

time: 1120 us -> 1370 us (1.22)
  blocking collectives: 75.8 us -> 472 us
  waiting for transfers between devices: 449 us -> 284 us
    unnamed x1, blocking collectives: 39.8 us -> 436 us
    all_gather x1 -> x0, waiting for transfers between devices: 163 us -> none  [local(): lax.all_gather(received_rows.reshape(group_count * capacity, feature_widt...]
  transfers between devices with their start and end apart: 4 -> 4, of which waited for: 4 -> 3; matrix products, arithmetic and copies ran while one was open for 2% -> 1% of each run, Pallas kernels for 0% -> 0%
where the time goes in v1:
time: 1370 us; the launch traced here: 1360 us
  blocking collectives  472 us (34%)
  other arithmetic  390 us (28%)
  waiting for transfers between devices  284 us (21%)
  matrix products  99 us (7%)
  local copies, waits for them, and re-layouts  67.1 us (5%)
  between operations  24.6 us (2%)
  starting transfers between devices  22 us (2%)
    unnamed x1, blocking collectives  436 us
    psum x2, waiting for transfers between devices, panel_rows_fetch(): return lax.psum(placed, 'tile')  277 us
    another operation x45, other arithmetic, local(): diagonal_factor = jnp.linalg.cholesky(diagonal_block)  248 us
    another operation x5, other arithmetic, local(): jax.scipy.linalg.solve_triangular(diagonal_factor, panel_block.T, lower=T...  121 us
    all_to_all x1, blocking collectives, side_by_side(): lax.all_to_all(both, axis, split_axis=split_dim, concat_axis=concat_dim,...  36 us
    another operation x39, local copies, waits for them, and re-layouts, local(): jax.scipy.linalg.solve_triangular(diagonal_factor, panel_block.T, lower=T...  35.3 us
  transfers between devices with their start and end apart: 4, of which 3 were waited for; matrix products, arithmetic and copies ran while one was open for 1% of the time, Pallas kernels for 0%

profile of v1, /device:TPU:0, one launch (start us, length us, event | category | flops | bytes accessed | tf_op | source)
XLA Modules:
  0.0 1359.8 jit_solution(16586376367905515183)
XLA Ops:
  9.4 36.0 %all_to_all.16 = bf16[8,24,6145]{2,1,0:T(8,128)(2,1)S(1)} all-to-all(bf16[8,24,6145]{2,1,0:T(8,128)(2,1)S(1)} %pad_maximum_fusion), channel_id=1, replica_groups=mesh['expert'=8,'tile'=16] {'expert'}, dimensions={0} | all-to-all | bytes 4719360 | tf_op jit(solution)/shard_map/all_to_all | solution.py:16
  45.6 12.5 stack.3
  67.8 436.4 %all-reduce.1 = bf16[3072]{0:T(1024)(128)(2,1)S(1)} all-reduce(bf16[3072]{0:T(1024)(128)(2,1)S(1)} %dynamic-update-slice.25), channel_id=1, replica_groups=mesh['expert'=8,'tile'=16] {'tile'}, use_global_device_ids=true, to_apply=%add.1 | all-reduce | flops 3072 | bytes 12288
  505.5 24.3 %select_reduce_fusion = (f32[]{:T(128)}, f32[384,6144]{1,0:T(8,128)}) fusion(s32[384]{0:T(512)S(1)} %iota_add_fusion.1, f32[]{:T(128)S(6)} %div.12, bf16[3072,6144]{1,0:T(8,128)(2,1)} %bitcast.3, s32[]{:T(128)S(6)} %select_n.21), kind=kOutput, calls=%fused_computation.5 | convolution fusion | flops 14504951808 | bytes 49546764 | tf_op jit(solution)/shard_map/tr,tc->rc/dot_general | solution.py:76
  555.3 10.6 all-reduce.8.cloned.1.call-start
  573.3 125.7 %all-reduce.6.cloned.1.call-done = f32[768,768]{0,1:T(8,128)} async-done(((f32[768,768]{0,1:T(8,128)}), f32[768,768]{0,1:T(8,128)}) %all-reduce.6.cloned.1.call-update) | async-done | bytes 2359312 | tf_op jit(solution)/shard_map/psum | solution.py:96
  705.6 11.7 cholesky.453
  730.1 11.7 cholesky.472
  741.8 10.2 custom-call.42
  754.0 11.7 cholesky.493
  778.1 11.9 cholesky.512
  802.3 11.7 cholesky.531
  826.0 12.1 cholesky.548
  844.8 17.5 %while.4 = (s32[]{:T(128)}, f32[768,768]{1,0:T(8,128)}, s32[6,2]{0,1:T(2,128)S(1)}, f32[6,128,128]{2,1,0:T(8,128)S(1)}, s32[]{:T(128)}) while((s32[]{:T(128)}, f32[768,768]{1,0:T(8,128)}, s32[6,2]{0,1:T(2,128)S(1)}, f32[6,128,128]{2,1,0:T(8,128)S(1)}, s32[]{:T(128)}) %tuple.86), condition=%wide.while_cond, body=%wide.while_body.sunk | while | flops 2 | bytes 131181 | solution.py:113
  862.4 59.0 %custom-call.46 = f32[6,128,128]{1,2,0:T(8,128)S(1)} custom-call(f32[6,128,128]{2,1,0:T(8,128)S(1)} %get-tuple-element.18), custom_call_target="InvertDiagBlocksLowerTriangular" | custom-call | tf_op jit(solution)/shard_map/jit(_solve_triangular)/triangular_solve | solution.py:113
  948.2 151.3 %all-reduce.8.cloned.1.call-done = (f32[768,768]{1,0:T(8,128)}, f32[768,768]{0,1:T(8,128)}) async-done(((f32[768,768]{1,0:T(8,128)}, f32[768,768]{0,1:T(8,128)}), (f32[768,768]{1,0:T(8,128)}, f32[768,768]{0,1:T(8,128)})) %all-reduce.8.cloned.1.call-update) | async-done | bytes 4718608 | tf_op jit(solution)/shard_map/psum | solution.py:96
  1120.0 11.7 cholesky.563
  1144.6 11.7 cholesky.582
  1169.8 11.7 cholesky.603
  1193.8 11.8 cholesky.622
  1218.0 11.7 cholesky.641
  1241.7 11.9 cholesky.658
  1259.5 17.9 %while.5 = (s32[]{:T(128)}, f32[768,768]{1,0:T(8,128)}, s32[6,2]{0,1:T(2,128)S(1)}, f32[6,128,128]{2,1,0:T(8,128)S(1)}, s32[]{:T(128)}) while((s32[]{:T(128)}, f32[768,768]{1,0:T(8,128)}, s32[6,2]{0,1:T(2,128)S(1)}, f32[6,128,128]{2,1,0:T(8,128)S(1)}, s32[]{:T(128)}) %tuple.97), condition=%wide.while_cond.clone, body=%wide.while_body.clone.sunk | while | flops 2 | bytes 131181 | solution.py:113
  1277.5 59.0 %custom-call.52 = f32[6,128,128]{1,2,0:T(8,128)S(1)} custom-call(f32[6,128,128]{2,1,0:T(8,128)S(1)} %get-tuple-element.19), custom_call_target="InvertDiagBlocksLowerTriangular" | custom-call | tf_op jit(solution)/shard_map/jit(_solve_triangular)/triangular_solve | solution.py:113
  (198 shorter events, 268.7 us)
Async XLA Ops:
  7.2 1.1 copy-start
  58.1 8.0 copy-start.12
  58.1 447.4 %all-to-all-start.1 = ((bf16[16,192,6144]{2,1,0:T(8,128)(2,1)}), bf16[16,192,6144]{2,1,0:T(8,128)(2,1)}, u32[]{:S(2)}, u32[]{:S(2)}) async-start(bf16[16,192,6144]{2,1,0:T(8,128)(2,1)} %stack.3), calls=%async_computation.1 | async-start | bytes 75497472 | tf_op jit(solution)/shard_map/all_to_all | solution.py:59
  531.0 10.9 all-to-all-start.2
  534.5 164.5 %all-reduce.6.cloned.1.call-start = ((), (), s32[]{:S(2)}) async-start(), calls=%async_computation.3 | async-start | bytes 4718592 | tf_op jit(solution)/shard_map/psum | solution.py:96
  548.1 3.6 copy-start.2
  555.3 544.2 %all-reduce.8.cloned.1.call-start = ((), (), s32[]{:S(2)}) async-start(), calls=%async_computation.4 | async-start | bytes 9437184 | tf_op jit(solution)/shard_map/psum | solution.py:96
  699.0 3.2 copy-start.6
  704.1 1.4 copy-start.8
  844.8 79.7 %copy-start.9 = (f32[768,384]{0,1:T(8,128)S(1)}, f32[768,384]{0,1:T(8,128)}, u32[]{:S(2)}) copy-start(f32[768,384]{0,1:T(8,128)} %slice_bitcast_fusion) | copy-start | bytes 3538948
  935.1 164.4 %copy-start.4 = (f32[384,768]{0,1:T(8,128)}, f32[384,768]{0,1:T(8,128)S(1)}, u32[]{:S(2)}) copy-start(f32[384,768]{0,1:T(8,128)S(1)} %bitcast_select_fusion.1) | copy-start | bytes 3538948
  1099.5 9.0 copy-start.3
  1099.5 9.0 copy-start.11
  1118.6 1.4 copy-start.7
  1259.5 80.1 %copy-start.10 = (f32[768,384]{0,1:T(8,128)S(1)}, f32[768,384]{0,1:T(8,128)}, u32[]{:S(2)}) copy-start(f32[768,384]{0,1:T(8,128)} %fusion.7) | copy-start | bytes 3538948
  1347.0 3.4 copy-start.5
  1350.4 2.1 copy-start.1
Sparse Core Ops, SparseCore 0:
  555.5 143.4 all-reduce.5
  938.8 160.6 all-reduce.7
